TPU v7x, 256 devices: a whole 4x4x8 slice. The times are simulated.
256 devices in a mesh: lx: 8 (over z), ly: 8 (over x, y_lo), blk: 4 (over y_hi, core).
Axes of the slice: x: 4, y: 4 (y_hi: 2, y_lo: 2; y = y_hi * 2 + y_lo), z: 8, core: 2. Of those that a mesh axis runs over, the one named last changes fastest.
Arguments:
- block_vectors: float32 [32, 1024, 2048], P('blk', 'lx', 'ly'), may hold values from -6 to 6
- search_vectors: float32 [256, 1024, 2048], P('blk', 'lx', 'ly'), may hold values from -6 to 6
- onsite_energy: float32 [1024, 2048], P('lx', 'ly'), may hold values from -1 to 1
- site_mask: int32 [1024, 2048], P('lx', 'ly'), may hold values 0 or 1
- filter_coefs: float32 [5], replicated, may hold values from -1 to 1
Outputs:
- projected: float32 [2, 32, 256], P(None, None, 'blk')
Inputs may be any that keep to these rules, and one draw needn't show every extreme that they name: `site_mask`: 1 marks a present site, 0 a vacancy.
All inputs are finite; a program needn't handle non-finite values. No bound on the sum of `site_mask` on one device may be relied on, other than what follows from the above.
Results may differ from a plain program's by a relative error of at most 0.00016.
Values sent between devices are 32-bit elements; how exact they have to be, the bound alone decides.
No kernel may reach another device: no remote copies, remote signals or barrier semaphores. Data moves between devices by JAX's collectives and lax.ppermute only.
A program may use at most 64 MiB of HBM per device.

v0:
```python
import math
import jax
import jax.numpy as jnp
from jax import lax
from jax.sharding import PartitionSpec as P


def extended(block, sides, width):
    for axis, dim in sides:
        count = lax.axis_size(axis)
        forward = [(i, i + 1) for i in range(count - 1)]
        backward = [(target, source) for source, target in forward]
        low = lax.ppermute(
            lax.slice_in_dim(block, block.shape[dim] - width, None, axis=dim), axis, forward
        )
        high = lax.ppermute(lax.slice_in_dim(block, 0, width, axis=dim), axis, backward)
        block = jnp.concatenate([low, block, high], axis=dim)
    return block


def scaled_step(padded, onsite, present):
    nrows, ncols = onsite.shape
    row_index = lax.broadcasted_iota(jnp.int32, (nrows, ncols), 0)
    col_index = lax.broadcasted_iota(jnp.int32, (nrows, ncols), 1)
    even_sites = (row_index + col_index) % 2 == 0
    centre = padded[..., 1:-1, 1:-1]
    left_side = padded[..., 1:-1, :-2]
    right_side = padded[..., 1:-1, 2:]
    upper_side = padded[..., :-2, 1:-1]
    lower_side = padded[..., 2:, 1:-1]
    vertical = jnp.where(even_sites, lower_side, upper_side)
    return present * (onsite * centre - (left_side + right_side + vertical)) * 0.25


def gram_rows(stacked, search_vectors):
    stacks, members, nrows, ncols = stacked.shape
    flat = stacked.reshape(stacks * members, nrows * ncols)
    search_flat = search_vectors.reshape(search_vectors.shape[0], nrows * ncols)
    result = lax.dot_general(
        flat,
        search_flat,
        (((1,), (1,)), ((), ())),
        precision=lax.Precision.HIGHEST,
        preferred_element_type=jnp.float32,
    )
    return result.reshape(stacks, members, search_vectors.shape[0])


def shards(block_vectors, search_vectors, onsite_energy, site_mask, filter_coefs):
    present = site_mask.astype(jnp.float32)
    current = block_vectors * present
    filtered = filter_coefs[0] * current
    degree = filter_coefs.shape[0] - 1
    before = current
    for order in range(1, degree + 1):
        padded_field = extended(current, (("lx", 1), ("ly", 2)), 1)
        image = scaled_step(padded_field, onsite_energy, present)
        following = image if order == 1 else 2.0 * image - before
        before, current = (current, following)
        filtered = filtered + filter_coefs[order] * current
    nrows, ncols = onsite_energy.shape
    scale_factor = 1.0 / math.sqrt(nrows * ncols * lax.axis_size("lx") * lax.axis_size("ly"))
    padded_field = extended(filtered, (("lx", 1), ("ly", 2)), 1)
    image = scaled_step(padded_field, onsite_energy, present)
    paired = jnp.stack([filtered, image])
    partial_gram = gram_rows(lax.all_gather(paired, "blk", axis=1, tiled=True), search_vectors)
    total = lax.psum(partial_gram, ("lx", "ly"))
    return total * scale_factor


def solution(mesh):
    placed = (P("blk", "lx", "ly"), P("blk", "lx", "ly"), P("lx", "ly"), P("lx", "ly"), P())
    return jax.shard_map(
        shards, mesh=mesh, in_specs=placed, out_specs=P(None, None, "blk"), check_vma=False
    )
```

profile of v0, /device:TPU:16, one launch (start us, length us, event | category | flops | bytes accessed | tf_op | source)
XLA Modules:
  0.0 537.4 jit_solution(5126460402475514423)
XLA Ops:
  6.5 0.9 convert_element_type.3
  7.5 1.8 copy_multiply_fusion
  9.3 1.3 collective-permute-start.1
  10.6 4.5 collective-permute-start
  15.2 1.3 collective-permute-done
  17.1 0.4 copy.11
  17.5 1.3 collective-permute-start.3
  18.8 4.5 collective-permute-start.2
  23.4 1.3 collective-permute-done.2
  24.7 1.2 copy.10
  25.9 1.2 copy.12
  27.1 1.9 broadcast_multiply_fusion
  29.0 1.3 collective-permute-start.5
  30.3 4.8 collective-permute-start.4
  35.2 1.3 collective-permute-done.4
  36.6 1.0 fusion.50
  37.6 1.4 copy.13
  39.0 0.4 copy.15
  39.3 1.3 collective-permute-start.7
  40.6 4.8 collective-permute-start.6
  45.5 0.7 broadcast_multiply_fusion.1
  46.1 0.7 collective-permute-done.6
  46.8 1.2 copy.14
  48.0 1.2 copy.16
  49.2 2.6 fusion.34
  51.8 1.3 collective-permute-start.9
  53.1 4.8 collective-permute-start.8
  58.0 1.3 collective-permute-done.8
  59.4 1.0 fusion.49
  60.4 1.4 copy.17
  61.8 5.0 collective-permute-start.10
  67.1 1.3 collective-permute-start.11
  68.4 0.4 copy.18
  68.8 5.0 collective-permute-done.11
  73.8 1.2 copy.20
  75.0 1.8 fusion.27
  76.8 1.3 collective-permute-start.13
  78.1 4.9 collective-permute-start.12
  83.1 1.3 collective-permute-done.12
  84.5 1.0 fusion.48
  85.5 1.4 copy.21
  86.9 0.4 copy.23
  87.2 1.3 collective-permute-start.15
  88.5 5.4 %collective-permute-start.14 = (f32[8,130,1]{1,0,2:T(8,128)S(1)}, f32[8,130,1]{1,0,2:T(8,128)S(1)}, u32[]{:S(2)}, u32[]{:S(2)}) collective-permute-start(f32[8,130,1]{1,0,2:T(8,128)S(1)} %copy.21), channel_id=1, source_target_pairs={{0,4},{4,8},{8,12},{12,16},{16,20},{20,24},{24,28},{1,5},{5,9},{9,... | collective-permute-start | bytes 12488 | tf_op jit(solution)/shard_map/ppermute | solution.py:13
  94.0 0.7 fusion.57
  95.3 1.2 copy.22
  96.5 1.2 copy.24
  97.7 8.3 %fusion.20 = f32[8,128,256]{2,0,1:T(8,128)S(1)} fusion(f32[8,128,256]{2,0,1:T(8,128)S(1)} %fusion.34, f32[8,128,256]{2,0,1:T(8,128)} %copy-done, f32[8,1,256]{2,0,1:T(8,128)S(1)} %collective-permute-done.12, f32[8,1,256]{2,0,1:T(8,128)S(1)} %collective-permute-done.13, f32[8,130,1]{2,0,1:T(8,128)} %copy.24, f32[8,130,1]{2,0,1:T(8,128)} %copy.22, ...), kind=kLoop, calls=%fused_computation.33 | loop fusion | flops 6815744 | bytes 5562516 | tf_op jit(solution)/shard_map/add | solution.py:60
  106.0 1.3 collective-permute-start.17
  107.3 6.0 %collective-permute-start.16 = (f32[8,1,256]{2,0,1:T(8,128)S(1)}, f32[8,1,256]{2,0,1:T(8,128)S(1)}, u32[]{:S(2)}, u32[]{:S(2)}) collective-permute-start(f32[8,1,256]{2,0,1:T(8,128)S(1)} %get-tuple-element.18), channel_id=1, source_target_pairs={{0,32},{32,64},{64,96},{96,128},{128,160},{160,192},{192,224},{1,3... | collective-permute-start | bytes 24584 | tf_op jit(solution)/shard_map/ppermute | solution.py:13
  113.3 1.3 collective-permute-done.16
  115.0 0.4 copy.25
  115.3 4.8 collective-permute-start.18
  120.1 0.3 copy.27
  120.5 1.5 collective-permute-start.19
  122.0 0.4 copy.26
  122.4 4.8 collective-permute-done.19
  127.2 1.2 copy.28
  128.4 1.8 fusion.11
  130.2 1.5 pad_maximum_fusion
  131.7 71.7 %all-gather.2.cloned.1.call-done = f32[2,32,128,256]{3,1,2,0:T(8,128)} async-done(((f32[2,8,128,256]{3,1,2,0:T(8,128)}), f32[2,32,128,256]{3,1,2,0:T(8,128)}) %all-gather.2.cloned.1.call-update) | async-done | bytes 8388624 | tf_op jit(solution)/shard_map/all_gather | solution.py:66
  203.4 16.7 %fusion.3 = f32[2,32,64]{2,1,0:T(8,128)S(1)} fusion(f32[2,32,128,256]{3,1,2,0:T(8,128)} %all-gather.2.cloned.1.call-done, f32[64,128,256]{2,1,0:T(8,128)} %param.6), kind=kOutput, calls=%fused_computation.4 | convolution fusion | flops 1610612736 | bytes 16793600 | tf_op jit(solution)/shard_map/dot_general | solution.py:39
  220.0 309.9 %psum.7 = f32[2,32,64]{2,1,0:T(8,128)S(1)} all-reduce(f32[2,32,64]{2,1,0:T(8,128)S(1)} %fusion.3), channel_id=1, replica_groups=mesh['lx'=8,'ly'=8,'blk'=4] {'lx','ly'}, use_global_device_ids=true, to_apply=%region_0.1 | all-reduce | flops 4096 | bytes 32768 | tf_op jit(solution)/shard_map/psum | solution.py:67
  529.9 0.6 broadcast_multiply_fusion.2
  (34 shorter events, 1.7 us)
Async XLA Ops:
  6.5 196.8 %all-gather.2.cloned.1.call-start = ((), (), s32[]{:S(2)}) async-start(), calls=%async_computation | async-start | bytes 10485760 | tf_op jit(solution)/shard_map/all_gather | solution.py:66
  9.3 5.9 %collective-permute-start.1 = (f32[8,1,256]{2,0,1:T(8,128)S(1)}, f32[8,1,256]{2,0,1:T(8,128)S(1)}, u32[]{:S(2)}, u32[]{:S(2)}) collective-permute-start(f32[8,1,256]{2,0,1:T(8,128)S(1)} %get-tuple-element.25), channel_id=1, source_target_pairs={{32,0},{64,32},{96,64},{128,96},{160,128},{192,160},{224,192},{33,... | collective-permute-start | bytes 24584 | tf_op jit(solution)/shard_map/ppermute | solution.py:16
  10.6 5.9 %collective-permute-start = (f32[8,1,256]{2,0,1:T(8,128)S(1)}, f32[8,1,256]{2,0,1:T(8,128)S(1)}, u32[]{:S(2)}, u32[]{:S(2)}) collective-permute-start(f32[8,1,256]{2,0,1:T(8,128)S(1)} %get-tuple-element.26), channel_id=1, source_target_pairs={{0,32},{32,64},{64,96},{96,128},{128,160},{160,192},{192,224},{1,3... | collective-permute-start | bytes 24584 | tf_op jit(solution)/shard_map/ppermute | solution.py:13
  16.8 10.3 %copy-start.1 = (f32[128,256]{1,0:T(8,128)S(1)}, f32[128,256]{1,0:T(8,128)}, u32[]{:S(2)}) copy-start(f32[128,256]{1,0:T(8,128)} %param.7) | copy-start | bytes 393220
  17.5 8.4 %collective-permute-start.3 = (f32[8,130,1]{1,0,2:T(8,128)S(1)}, f32[8,130,1]{1,0,2:T(8,128)S(1)}, u32[]{:S(2)}, u32[]{:S(2)}) collective-permute-start(f32[8,130,1]{1,0,2:T(8,128)S(1)} %copy.11), channel_id=1, source_target_pairs={{4,0},{8,4},{12,8},{16,12},{20,16},{24,20},{28,24},{5,1},{9,5},{13... | collective-permute-start | bytes 12488 | tf_op jit(solution)/shard_map/ppermute | solution.py:16
  18.8 5.9 %collective-permute-start.2 = (f32[8,130,1]{1,0,2:T(8,128)S(1)}, f32[8,130,1]{1,0,2:T(8,128)S(1)}, u32[]{:S(2)}, u32[]{:S(2)}) collective-permute-start(f32[8,130,1]{1,0,2:T(8,128)S(1)} %copy.9), channel_id=1, source_target_pairs={{0,4},{4,8},{8,12},{12,16},{16,20},{20,24},{24,28},{1,5},{5,9},{9,... | collective-permute-start | bytes 12488 | tf_op jit(solution)/shard_map/ppermute | solution.py:13
  29.0 6.1 %collective-permute-start.5 = (f32[8,1,256]{2,0,1:T(8,128)S(1)}, f32[8,1,256]{2,0,1:T(8,128)S(1)}, u32[]{:S(2)}, u32[]{:S(2)}) collective-permute-start(f32[8,1,256]{2,0,1:T(8,128)S(1)} %get-tuple-element.23), channel_id=1, source_target_pairs={{32,0},{64,32},{96,64},{128,96},{160,128},{192,160},{224,192},{33,... | collective-permute-start | bytes 24584 | tf_op jit(solution)/shard_map/ppermute | solution.py:16
  30.3 6.2 %collective-permute-start.4 = (f32[8,1,256]{2,0,1:T(8,128)S(1)}, f32[8,1,256]{2,0,1:T(8,128)S(1)}, u32[]{:S(2)}, u32[]{:S(2)}) collective-permute-start(f32[8,1,256]{2,0,1:T(8,128)S(1)} %get-tuple-element.24), channel_id=1, source_target_pairs={{0,32},{32,64},{64,96},{96,128},{128,160},{160,192},{192,224},{1,3... | collective-permute-start | bytes 24584 | tf_op jit(solution)/shard_map/ppermute | solution.py:13
  39.3 8.7 %collective-permute-start.7 = (f32[8,130,1]{1,0,2:T(8,128)S(1)}, f32[8,130,1]{1,0,2:T(8,128)S(1)}, u32[]{:S(2)}, u32[]{:S(2)}) collective-permute-start(f32[8,130,1]{1,0,2:T(8,128)S(1)} %copy.15), channel_id=1, source_target_pairs={{4,0},{8,4},{12,8},{16,12},{20,16},{24,20},{28,24},{5,1},{9,5},{13... | collective-permute-start | bytes 12488 | tf_op jit(solution)/shard_map/ppermute | solution.py:16
  40.6 6.2 %collective-permute-start.6 = (f32[8,130,1]{1,0,2:T(8,128)S(1)}, f32[8,130,1]{1,0,2:T(8,128)S(1)}, u32[]{:S(2)}, u32[]{:S(2)}) collective-permute-start(f32[8,130,1]{1,0,2:T(8,128)S(1)} %copy.13), channel_id=1, source_target_pairs={{0,4},{4,8},{8,12},{12,16},{16,20},{20,24},{24,28},{1,5},{5,9},{9,... | collective-permute-start | bytes 12488 | tf_op jit(solution)/shard_map/ppermute | solution.py:13
  51.8 6.1 %collective-permute-start.9 = (f32[8,1,256]{2,0,1:T(8,128)S(1)}, f32[8,1,256]{2,0,1:T(8,128)S(1)}, u32[]{:S(2)}, u32[]{:S(2)}) collective-permute-start(f32[8,1,256]{2,0,1:T(8,128)S(1)} %get-tuple-element.21), channel_id=1, source_target_pairs={{32,0},{64,32},{96,64},{128,96},{160,128},{192,160},{224,192},{33,... | collective-permute-start | bytes 24584 | tf_op jit(solution)/shard_map/ppermute | solution.py:16
  53.1 6.2 %collective-permute-start.8 = (f32[8,1,256]{2,0,1:T(8,128)S(1)}, f32[8,1,256]{2,0,1:T(8,128)S(1)}, u32[]{:S(2)}, u32[]{:S(2)}) collective-permute-start(f32[8,1,256]{2,0,1:T(8,128)S(1)} %get-tuple-element.22), channel_id=1, source_target_pairs={{0,32},{32,64},{64,96},{96,128},{128,160},{160,192},{192,224},{1,3... | collective-permute-start | bytes 24584 | tf_op jit(solution)/shard_map/ppermute | solution.py:13
  61.8 6.6 %collective-permute-start.10 = (f32[8,130,1]{1,0,2:T(8,128)S(1)}, f32[8,130,1]{1,0,2:T(8,128)S(1)}, u32[]{:S(2)}, u32[]{:S(2)}) collective-permute-start(f32[8,130,1]{1,0,2:T(8,128)S(1)} %copy.17), channel_id=1, source_target_pairs={{0,4},{4,8},{8,12},{12,16},{16,20},{20,24},{24,28},{1,5},{5,9},{9,... | collective-permute-start | bytes 12488 | tf_op jit(solution)/shard_map/ppermute | solution.py:13
  67.1 6.7 %collective-permute-start.11 = (f32[8,130,1]{1,0,2:T(8,128)S(1)}, f32[8,130,1]{1,0,2:T(8,128)S(1)}, u32[]{:S(2)}, u32[]{:S(2)}) collective-permute-start(f32[8,130,1]{1,0,2:T(8,128)S(1)} %copy.19), channel_id=1, source_target_pairs={{4,0},{8,4},{12,8},{16,12},{20,16},{24,20},{28,24},{5,1},{9,5},{13... | collective-permute-start | bytes 12488 | tf_op jit(solution)/shard_map/ppermute | solution.py:16
  76.8 7.7 %copy-start = (f32[8,128,256]{2,0,1:T(8,128)}, f32[8,128,256]{2,0,1:T(8,128)S(1)}, u32[]{:S(2)}) copy-start(f32[8,128,256]{2,0,1:T(8,128)S(1)} %fusion.27) | copy-start | bytes 3145732
  76.8 6.2 %collective-permute-start.13 = (f32[8,1,256]{2,0,1:T(8,128)S(1)}, f32[8,1,256]{2,0,1:T(8,128)S(1)}, u32[]{:S(2)}, u32[]{:S(2)}) collective-permute-start(f32[8,1,256]{2,0,1:T(8,128)S(1)} %get-tuple-element.19), channel_id=1, source_target_pairs={{32,0},{64,32},{96,64},{128,96},{160,128},{192,160},{224,192},{33,... | collective-permute-start | bytes 24584 | tf_op jit(solution)/shard_map/ppermute | solution.py:16
  78.1 6.3 %collective-permute-start.12 = (f32[8,1,256]{2,0,1:T(8,128)S(1)}, f32[8,1,256]{2,0,1:T(8,128)S(1)}, u32[]{:S(2)}, u32[]{:S(2)}) collective-permute-start(f32[8,1,256]{2,0,1:T(8,128)S(1)} %get-tuple-element.20), channel_id=1, source_target_pairs={{0,32},{32,64},{64,96},{96,128},{128,160},{160,192},{192,224},{1,3... | collective-permute-start | bytes 24584 | tf_op jit(solution)/shard_map/ppermute | solution.py:13
  85.5 8.5 %copy-start.2 = (f32[5]{0:T(128)S(1)}, f32[5]{0:T(128)}, u32[]{:S(2)}) copy-start(f32[5]{0:T(128)} %param.9) | copy-start | bytes 64
  87.2 9.3 %collective-permute-start.15 = (f32[8,130,1]{1,0,2:T(8,128)S(1)}, f32[8,130,1]{1,0,2:T(8,128)S(1)}, u32[]{:S(2)}, u32[]{:S(2)}) collective-permute-start(f32[8,130,1]{1,0,2:T(8,128)S(1)} %copy.23), channel_id=1, source_target_pairs={{4,0},{8,4},{12,8},{16,12},{20,16},{24,20},{28,24},{5,1},{9,5},{13... | collective-permute-start | bytes 12488 | tf_op jit(solution)/shard_map/ppermute | solution.py:16
  88.5 6.8 %collective-permute-start.14 = (f32[8,130,1]{1,0,2:T(8,128)S(1)}, f32[8,130,1]{1,0,2:T(8,128)S(1)}, u32[]{:S(2)}, u32[]{:S(2)}) collective-permute-start(f32[8,130,1]{1,0,2:T(8,128)S(1)} %copy.21), channel_id=1, source_target_pairs={{0,4},{4,8},{8,12},{12,16},{16,20},{20,24},{24,28},{1,5},{5,9},{9,... | collective-permute-start | bytes 12488 | tf_op jit(solution)/shard_map/ppermute | solution.py:13
  106.0 7.3 %collective-permute-start.17 = (f32[8,1,256]{2,0,1:T(8,128)S(1)}, f32[8,1,256]{2,0,1:T(8,128)S(1)}, u32[]{:S(2)}, u32[]{:S(2)}) collective-permute-start(f32[8,1,256]{2,0,1:T(8,128)S(1)} %get-tuple-element.17), channel_id=1, source_target_pairs={{32,0},{64,32},{96,64},{128,96},{160,128},{192,160},{224,192},{33,... | collective-permute-start | bytes 24584 | tf_op jit(solution)/shard_map/ppermute | solution.py:16
  107.3 7.4 %collective-permute-start.16 = (f32[8,1,256]{2,0,1:T(8,128)S(1)}, f32[8,1,256]{2,0,1:T(8,128)S(1)}, u32[]{:S(2)}, u32[]{:S(2)}) collective-permute-start(f32[8,1,256]{2,0,1:T(8,128)S(1)} %get-tuple-element.18), channel_id=1, source_target_pairs={{0,32},{32,64},{64,96},{96,128},{128,160},{160,192},{192,224},{1,3... | collective-permute-start | bytes 24584 | tf_op jit(solution)/shard_map/ppermute | solution.py:13
  115.3 6.7 %collective-permute-start.18 = (f32[8,130,1]{1,0,2:T(8,128)S(1)}, f32[8,130,1]{1,0,2:T(8,128)S(1)}, u32[]{:S(2)}, u32[]{:S(2)}) collective-permute-start(f32[8,130,1]{1,0,2:T(8,128)S(1)} %copy.25), channel_id=1, source_target_pairs={{0,4},{4,8},{8,12},{12,16},{16,20},{20,24},{24,28},{1,5},{5,9},{9,... | collective-permute-start | bytes 12488 | tf_op jit(solution)/shard_map/ppermute | solution.py:13
  120.5 6.7 %collective-permute-start.19 = (f32[8,130,1]{1,0,2:T(8,128)S(1)}, f32[8,130,1]{1,0,2:T(8,128)S(1)}, u32[]{:S(2)}, u32[]{:S(2)}) collective-permute-start(f32[8,130,1]{1,0,2:T(8,128)S(1)} %copy.27), channel_id=1, source_target_pairs={{4,0},{8,4},{12,8},{16,12},{20,16},{24,20},{28,24},{5,1},{9,5},{13... | collective-permute-start | bytes 12488 | tf_op jit(solution)/shard_map/ppermute | solution.py:16
Sparse Core Ops, SparseCore 0:
  131.8 71.4 all-gather.1
where the time goes:
time: 538 us; the launch traced here: 537 us
  blocking collectives  310 us (58%)
  waiting for transfers between devices  90.3 us (17%)
  starting transfers between devices  62.9 us (12%)
  other arithmetic  22.4 us (4%)
  local copies, waits for them, and re-layouts  20.9 us (4%)
  matrix products  16.7 us (3%)
  between operations  14.3 us (3%)
    psum x1, blocking collectives, shards(): total = lax.psum(partial_gram, ('lx', 'ly'))  310 us
    all_gather x1, waiting for transfers between devices, shards(): lax.all_gather(paired, 'blk', axis=1, tiled=True)  71.7 us
    ppermute x10, starting transfers between devices, extended(): lax.ppermute(lax.slice_in_dim(block, block.shape[dim] - width, None, axis...  49.7 us
    dot_general x1, matrix products, gram_rows(): lax.dot_general(flat, search_flat, (((1,), (1,)), ((), ())), precision=la...  16.7 us
    ppermute x10, starting transfers between devices, extended(): lax.ppermute(lax.slice_in_dim(block, 0, width, axis=dim), axis, backward)  13.1 us
  transfers between devices with their start and end apart: 21, of which 11 were waited for; matrix products, arithmetic and copies ran while one was open for 1% of the time, Pallas kernels for 0%

commit v1 on v0

--- a/solution.py
+++ b/solution.py
@@ -64,7 +64,7 @@
     image = scaled_step(padded_field, onsite_energy, present)
     paired = jnp.stack([filtered, image])
     partial_gram = gram_rows(lax.all_gather(paired, "blk", axis=1, tiled=True), search_vectors)
-    total = lax.psum(partial_gram, ("lx", "ly"))
+    total = lax.psum(lax.psum(partial_gram, "lx"), "ly")
     return total * scale_factor
 
 

time: 538 us -> 294 us (0.55)
  blocking collectives: 310 us -> 65.1 us
    psum x1 -> x2, blocking collectives: 310 us -> 65.1 us  [shards(): total = lax.psum(lax.psum(partial_gram, 'lx'), 'ly')]
  transfers between devices with their start and end apart: 21 -> 21, of which waited for: 11 -> 10; matrix products, arithmetic and copies ran while one was open for 1% -> 2% of each run, Pallas kernels for 0% -> 0%
where the time goes in v1:
time: 294 us; the launch traced here: 293 us
  waiting for transfers between devices  90.2 us (31%)
  blocking collectives  65.1 us (22%)
  starting transfers between devices  62.9 us (21%)
  other arithmetic  22.4 us (8%)
  local copies, waits for them, and re-layouts  21 us (7%)
  matrix products  16.7 us (6%)
  between operations  14.4 us (5%)
    all_gather x1, waiting for transfers between devices, shards(): lax.all_gather(paired, 'blk', axis=1, tiled=True)  71.7 us
    psum x2, blocking collectives, shards(): total = lax.psum(lax.psum(partial_gram, 'lx'), 'ly')  65.1 us
    ppermute x10, starting transfers between devices, extended(): lax.ppermute(lax.slice_in_dim(block, block.shape[dim] - width, None, axis...  49.7 us
    dot_general x1, matrix products, gram_rows(): lax.dot_general(flat, search_flat, (((1,), (1,)), ((), ())), precision=la...  16.7 us
    ppermute x10, starting transfers between devices, extended(): lax.ppermute(lax.slice_in_dim(block, 0, width, axis=dim), axis, backward)  13.1 us
    ppermute x10, waiting for transfers between devices, extended(): lax.ppermute(lax.slice_in_dim(block, 0, width, axis=dim), axis, backward)  9.85 us
    ppermute x10, waiting for transfers between devices, extended(): lax.ppermute(lax.slice_in_dim(block, block.shape[dim] - width, None, axis...  8.71 us
    add x1, other arithmetic, shards(): filtered = filtered + filter_coefs[order] * current  8.34 us
  transfers between devices with their start and end apart: 21, of which 10 were waited for; matrix products, arithmetic and copies ran while one was open for 2% of the time, Pallas kernels for 0%

profile of v1, /device:TPU:16, one launch (start us, length us, event | category | flops | bytes accessed | tf_op | source)
XLA Modules:
  0.0 292.8 jit_solution(2122486373261042074)
XLA Ops:
  6.5 0.9 convert_element_type.3
  7.5 1.8 copy_multiply_fusion
  9.3 1.3 collective-permute-start.1
  10.6 4.5 %collective-permute-start = (f32[8,1,256]{2,0,1:T(8,128)S(1)}, f32[8,1,256]{2,0,1:T(8,128)S(1)}, u32[]{:S(2)}, u32[]{:S(2)}) collective-permute-start(f32[8,1,256]{2,0,1:T(8,128)S(1)} %get-tuple-element.26), channel_id=1, source_target_pairs={{0,32},{32,64},{64,96},{96,128},{128,160},{160,192},{192,224},{1,3... | collective-permute-start | bytes 24584 | tf_op jit(solution)/shard_map/ppermute | solution.py:13
  15.2 1.3 collective-permute-done
  17.1 0.4 copy.11
  17.5 1.3 collective-permute-start.3
  18.8 4.5 %collective-permute-start.2 = (f32[8,130,1]{1,0,2:T(8,128)S(1)}, f32[8,130,1]{1,0,2:T(8,128)S(1)}, u32[]{:S(2)}, u32[]{:S(2)}) collective-permute-start(f32[8,130,1]{1,0,2:T(8,128)S(1)} %copy.9), channel_id=1, source_target_pairs={{0,4},{4,8},{8,12},{12,16},{16,20},{20,24},{24,28},{1,5},{5,9},{9,... | collective-permute-start | bytes 12488 | tf_op jit(solution)/shard_map/ppermute | solution.py:13
  23.4 1.3 collective-permute-done.2
  24.7 1.2 copy.10
  25.9 1.2 copy.12
  27.1 1.9 broadcast_multiply_fusion
  29.1 1.3 collective-permute-start.5
  30.4 4.8 %collective-permute-start.4 = (f32[8,1,256]{2,0,1:T(8,128)S(1)}, f32[8,1,256]{2,0,1:T(8,128)S(1)}, u32[]{:S(2)}, u32[]{:S(2)}) collective-permute-start(f32[8,1,256]{2,0,1:T(8,128)S(1)} %get-tuple-element.24), channel_id=1, source_target_pairs={{0,32},{32,64},{64,96},{96,128},{128,160},{160,192},{192,224},{1,3... | collective-permute-start | bytes 24584 | tf_op jit(solution)/shard_map/ppermute | solution.py:13
  35.2 1.3 collective-permute-done.4
  36.6 1.0 fusion.50
  37.6 1.4 copy.13
  39.0 0.4 copy.15
  39.4 1.3 collective-permute-start.7
  40.7 4.8 %collective-permute-start.6 = (f32[8,130,1]{1,0,2:T(8,128)S(1)}, f32[8,130,1]{1,0,2:T(8,128)S(1)}, u32[]{:S(2)}, u32[]{:S(2)}) collective-permute-start(f32[8,130,1]{1,0,2:T(8,128)S(1)} %copy.13), channel_id=1, source_target_pairs={{0,4},{4,8},{8,12},{12,16},{16,20},{20,24},{24,28},{1,5},{5,9},{9,... | collective-permute-start | bytes 12488 | tf_op jit(solution)/shard_map/ppermute | solution.py:13
  45.5 0.7 broadcast_multiply_fusion.1
  46.1 0.7 collective-permute-done.6
  46.8 1.2 copy.14
  48.0 1.2 copy.16
  49.2 2.6 fusion.34
  51.8 1.3 collective-permute-start.9
  53.1 4.8 %collective-permute-start.8 = (f32[8,1,256]{2,0,1:T(8,128)S(1)}, f32[8,1,256]{2,0,1:T(8,128)S(1)}, u32[]{:S(2)}, u32[]{:S(2)}) collective-permute-start(f32[8,1,256]{2,0,1:T(8,128)S(1)} %get-tuple-element.22), channel_id=1, source_target_pairs={{0,32},{32,64},{64,96},{96,128},{128,160},{160,192},{192,224},{1,3... | collective-permute-start | bytes 24584 | tf_op jit(solution)/shard_map/ppermute | solution.py:13
  58.0 1.3 collective-permute-done.8
  59.4 1.0 fusion.49
  60.4 1.4 copy.17
  61.8 5.0 %collective-permute-start.10 = (f32[8,130,1]{1,0,2:T(8,128)S(1)}, f32[8,130,1]{1,0,2:T(8,128)S(1)}, u32[]{:S(2)}, u32[]{:S(2)}) collective-permute-start(f32[8,130,1]{1,0,2:T(8,128)S(1)} %copy.17), channel_id=1, source_target_pairs={{0,4},{4,8},{8,12},{12,16},{16,20},{20,24},{24,28},{1,5},{5,9},{9,... | collective-permute-start | bytes 12488 | tf_op jit(solution)/shard_map/ppermute | solution.py:13
  67.1 1.3 collective-permute-start.11
  68.4 0.4 copy.18
  68.8 5.0 %collective-permute-done.11 = f32[8,130,1]{1,0,2:T(8,128)S(1)} collective-permute-done((f32[8,130,1]{1,0,2:T(8,128)S(1)}, f32[8,130,1]{1,0,2:T(8,128)S(1)}, u32[]{:S(2)}, u32[]{:S(2)}) %collective-permute-start.11) | collective-permute-done | bytes 4192 | tf_op jit(solution)/shard_map/ppermute | solution.py:16
  73.9 1.2 copy.20
  75.0 1.8 fusion.27
  76.8 1.3 collective-permute-start.13
  78.2 4.9 %collective-permute-start.12 = (f32[8,1,256]{2,0,1:T(8,128)S(1)}, f32[8,1,256]{2,0,1:T(8,128)S(1)}, u32[]{:S(2)}, u32[]{:S(2)}) collective-permute-start(f32[8,1,256]{2,0,1:T(8,128)S(1)} %get-tuple-element.20), channel_id=1, source_target_pairs={{0,32},{32,64},{64,96},{96,128},{128,160},{160,192},{192,224},{1,3... | collective-permute-start | bytes 24584 | tf_op jit(solution)/shard_map/ppermute | solution.py:13
  83.1 1.3 collective-permute-done.12
  84.5 1.0 fusion.48
  85.5 1.4 copy.21
  86.9 0.4 copy.23
  87.3 1.3 collective-permute-start.15
  88.6 5.4 %collective-permute-start.14 = (f32[8,130,1]{1,0,2:T(8,128)S(1)}, f32[8,130,1]{1,0,2:T(8,128)S(1)}, u32[]{:S(2)}, u32[]{:S(2)}) collective-permute-start(f32[8,130,1]{1,0,2:T(8,128)S(1)} %copy.21), channel_id=1, source_target_pairs={{0,4},{4,8},{8,12},{12,16},{16,20},{20,24},{24,28},{1,5},{5,9},{9,... | collective-permute-start | bytes 12488 | tf_op jit(solution)/shard_map/ppermute | solution.py:13
  94.1 0.7 fusion.57
  95.4 1.2 copy.22
  96.6 1.2 copy.24
  97.7 8.3 %fusion.20 = f32[8,128,256]{2,0,1:T(8,128)S(1)} fusion(f32[8,128,256]{2,0,1:T(8,128)S(1)} %fusion.34, f32[8,128,256]{2,0,1:T(8,128)} %copy-done, f32[8,1,256]{2,0,1:T(8,128)S(1)} %collective-permute-done.12, f32[8,1,256]{2,0,1:T(8,128)S(1)} %collective-permute-done.13, f32[8,130,1]{2,0,1:T(8,128)} %copy.24, f32[8,130,1]{2,0,1:T(8,128)} %copy.22, ...), kind=kLoop, calls=%fused_computation.33 | loop fusion | flops 6815744 | bytes 5562516 | tf_op jit(solution)/shard_map/add | solution.py:60
  106.1 1.3 collective-permute-start.17
  107.4 6.0 %collective-permute-start.16 = (f32[8,1,256]{2,0,1:T(8,128)S(1)}, f32[8,1,256]{2,0,1:T(8,128)S(1)}, u32[]{:S(2)}, u32[]{:S(2)}) collective-permute-start(f32[8,1,256]{2,0,1:T(8,128)S(1)} %get-tuple-element.18), channel_id=1, source_target_pairs={{0,32},{32,64},{64,96},{96,128},{128,160},{160,192},{192,224},{1,3... | collective-permute-start | bytes 24584 | tf_op jit(solution)/shard_map/ppermute | solution.py:13
  113.5 1.3 collective-permute-done.16
  115.1 0.4 copy.25
  115.4 4.8 %collective-permute-start.18 = (f32[8,130,1]{1,0,2:T(8,128)S(1)}, f32[8,130,1]{1,0,2:T(8,128)S(1)}, u32[]{:S(2)}, u32[]{:S(2)}) collective-permute-start(f32[8,130,1]{1,0,2:T(8,128)S(1)} %copy.25), channel_id=1, source_target_pairs={{0,4},{4,8},{8,12},{12,16},{16,20},{20,24},{24,28},{1,5},{5,9},{9,... | collective-permute-start | bytes 12488 | tf_op jit(solution)/shard_map/ppermute | solution.py:13
  120.6 1.5 collective-permute-start.19
  122.1 0.4 copy.26
  122.5 4.8 %collective-permute-done.19 = f32[8,130,1]{1,0,2:T(8,128)S(1)} collective-permute-done((f32[8,130,1]{1,0,2:T(8,128)S(1)}, f32[8,130,1]{1,0,2:T(8,128)S(1)}, u32[]{:S(2)}, u32[]{:S(2)}) %collective-permute-start.19) | collective-permute-done | bytes 4192 | tf_op jit(solution)/shard_map/ppermute | solution.py:16
  127.3 1.2 copy.28
  128.5 1.8 fusion.11
  130.3 1.5 pad_maximum_fusion
  131.8 71.7 %all-gather.2.cloned.1.call-done = f32[2,32,128,256]{3,1,2,0:T(8,128)} async-done(((f32[2,8,128,256]{3,1,2,0:T(8,128)}), f32[2,32,128,256]{3,1,2,0:T(8,128)}) %all-gather.2.cloned.1.call-update) | async-done | bytes 8388624 | tf_op jit(solution)/shard_map/all_gather | solution.py:66
  203.5 16.7 %fusion.3 = f32[2,32,64]{2,1,0:T(8,128)S(1)} fusion(f32[2,32,128,256]{3,1,2,0:T(8,128)} %all-gather.2.cloned.1.call-done, f32[64,128,256]{2,1,0:T(8,128)} %param.6), kind=kOutput, calls=%fused_computation.4 | convolution fusion | flops 1610612736 | bytes 16793600 | tf_op jit(solution)/shard_map/dot_general | solution.py:39
  220.2 30.4 %psum.14 = f32[2,32,64]{2,1,0:T(8,128)S(1)} all-reduce(f32[2,32,64]{2,1,0:T(8,128)S(1)} %fusion.3), channel_id=1, replica_groups=mesh['lx'=8,'ly'=8,'blk'=4] {'lx'}, use_global_device_ids=true, to_apply=%region_0.1 | all-reduce | flops 4096 | bytes 32768 | tf_op jit(solution)/shard_map/psum | solution.py:67
  250.6 34.7 %psum.15 = f32[2,32,64]{2,1,0:T(8,128)S(1)} all-reduce(f32[2,32,64]{2,1,0:T(8,128)S(1)} %psum.14), channel_id=1, replica_groups=mesh['lx'=8,'ly'=8,'blk'=4] {'ly'}, use_global_device_ids=true, to_apply=%region_1.2 | all-reduce | flops 4096 | bytes 32768 | tf_op jit(solution)/shard_map/psum | solution.py:67
  285.3 0.6 broadcast_multiply_fusion.2
  (35 shorter events, 1.9 us)
Async XLA Ops:
  6.5 197.0 %all-gather.2.cloned.1.call-start = ((), (), s32[]{:S(2)}) async-start(), calls=%async_computation | async-start | bytes 10485760 | tf_op jit(solution)/shard_map/all_gather | solution.py:66
  9.3 5.9 %collective-permute-start.1 = (f32[8,1,256]{2,0,1:T(8,128)S(1)}, f32[8,1,256]{2,0,1:T(8,128)S(1)}, u32[]{:S(2)}, u32[]{:S(2)}) collective-permute-start(f32[8,1,256]{2,0,1:T(8,128)S(1)} %get-tuple-element.25), channel_id=1, source_target_pairs={{32,0},{64,32},{96,64},{128,96},{160,128},{192,160},{224,192},{33,... | collective-permute-start | bytes 24584 | tf_op jit(solution)/shard_map/ppermute | solution.py:16
  10.6 5.9 %collective-permute-start = (f32[8,1,256]{2,0,1:T(8,128)S(1)}, f32[8,1,256]{2,0,1:T(8,128)S(1)}, u32[]{:S(2)}, u32[]{:S(2)}) collective-permute-start(f32[8,1,256]{2,0,1:T(8,128)S(1)} %get-tuple-element.26), channel_id=1, source_target_pairs={{0,32},{32,64},{64,96},{96,128},{128,160},{160,192},{192,224},{1,3... | collective-permute-start | bytes 24584 | tf_op jit(solution)/shard_map/ppermute | solution.py:13
  16.8 10.3 %copy-start.1 = (f32[128,256]{1,0:T(8,128)S(1)}, f32[128,256]{1,0:T(8,128)}, u32[]{:S(2)}) copy-start(f32[128,256]{1,0:T(8,128)} %param.7) | copy-start | bytes 393220
  17.5 8.4 %collective-permute-start.3 = (f32[8,130,1]{1,0,2:T(8,128)S(1)}, f32[8,130,1]{1,0,2:T(8,128)S(1)}, u32[]{:S(2)}, u32[]{:S(2)}) collective-permute-start(f32[8,130,1]{1,0,2:T(8,128)S(1)} %copy.11), channel_id=1, source_target_pairs={{4,0},{8,4},{12,8},{16,12},{20,16},{24,20},{28,24},{5,1},{9,5},{13... | collective-permute-start | bytes 12488 | tf_op jit(solution)/shard_map/ppermute | solution.py:16
  18.8 5.9 %collective-permute-start.2 = (f32[8,130,1]{1,0,2:T(8,128)S(1)}, f32[8,130,1]{1,0,2:T(8,128)S(1)}, u32[]{:S(2)}, u32[]{:S(2)}) collective-permute-start(f32[8,130,1]{1,0,2:T(8,128)S(1)} %copy.9), channel_id=1, source_target_pairs={{0,4},{4,8},{8,12},{12,16},{16,20},{20,24},{24,28},{1,5},{5,9},{9,... | collective-permute-start | bytes 12488 | tf_op jit(solution)/shard_map/ppermute | solution.py:13
  29.1 6.1 %collective-permute-start.5 = (f32[8,1,256]{2,0,1:T(8,128)S(1)}, f32[8,1,256]{2,0,1:T(8,128)S(1)}, u32[]{:S(2)}, u32[]{:S(2)}) collective-permute-start(f32[8,1,256]{2,0,1:T(8,128)S(1)} %get-tuple-element.23), channel_id=1, source_target_pairs={{32,0},{64,32},{96,64},{128,96},{160,128},{192,160},{224,192},{33,... | collective-permute-start | bytes 24584 | tf_op jit(solution)/shard_map/ppermute | solution.py:16
  30.4 6.2 %collective-permute-start.4 = (f32[8,1,256]{2,0,1:T(8,128)S(1)}, f32[8,1,256]{2,0,1:T(8,128)S(1)}, u32[]{:S(2)}, u32[]{:S(2)}) collective-permute-start(f32[8,1,256]{2,0,1:T(8,128)S(1)} %get-tuple-element.24), channel_id=1, source_target_pairs={{0,32},{32,64},{64,96},{96,128},{128,160},{160,192},{192,224},{1,3... | collective-permute-start | bytes 24584 | tf_op jit(solution)/shard_map/ppermute | solution.py:13
  39.4 8.7 %collective-permute-start.7 = (f32[8,130,1]{1,0,2:T(8,128)S(1)}, f32[8,130,1]{1,0,2:T(8,128)S(1)}, u32[]{:S(2)}, u32[]{:S(2)}) collective-permute-start(f32[8,130,1]{1,0,2:T(8,128)S(1)} %copy.15), channel_id=1, source_target_pairs={{4,0},{8,4},{12,8},{16,12},{20,16},{24,20},{28,24},{5,1},{9,5},{13... | collective-permute-start | bytes 12488 | tf_op jit(solution)/shard_map/ppermute | solution.py:16
  40.7 6.2 %collective-permute-start.6 = (f32[8,130,1]{1,0,2:T(8,128)S(1)}, f32[8,130,1]{1,0,2:T(8,128)S(1)}, u32[]{:S(2)}, u32[]{:S(2)}) collective-permute-start(f32[8,130,1]{1,0,2:T(8,128)S(1)} %copy.13), channel_id=1, source_target_pairs={{0,4},{4,8},{8,12},{12,16},{16,20},{20,24},{24,28},{1,5},{5,9},{9,... | collective-permute-start | bytes 12488 | tf_op jit(solution)/shard_map/ppermute | solution.py:13
  51.8 6.1 %collective-permute-start.9 = (f32[8,1,256]{2,0,1:T(8,128)S(1)}, f32[8,1,256]{2,0,1:T(8,128)S(1)}, u32[]{:S(2)}, u32[]{:S(2)}) collective-permute-start(f32[8,1,256]{2,0,1:T(8,128)S(1)} %get-tuple-element.21), channel_id=1, source_target_pairs={{32,0},{64,32},{96,64},{128,96},{160,128},{192,160},{224,192},{33,... | collective-permute-start | bytes 24584 | tf_op jit(solution)/shard_map/ppermute | solution.py:16
  53.1 6.2 %collective-permute-start.8 = (f32[8,1,256]{2,0,1:T(8,128)S(1)}, f32[8,1,256]{2,0,1:T(8,128)S(1)}, u32[]{:S(2)}, u32[]{:S(2)}) collective-permute-start(f32[8,1,256]{2,0,1:T(8,128)S(1)} %get-tuple-element.22), channel_id=1, source_target_pairs={{0,32},{32,64},{64,96},{96,128},{128,160},{160,192},{192,224},{1,3... | collective-permute-start | bytes 24584 | tf_op jit(solution)/shard_map/ppermute | solution.py:13
  61.8 6.6 %collective-permute-start.10 = (f32[8,130,1]{1,0,2:T(8,128)S(1)}, f32[8,130,1]{1,0,2:T(8,128)S(1)}, u32[]{:S(2)}, u32[]{:S(2)}) collective-permute-start(f32[8,130,1]{1,0,2:T(8,128)S(1)} %copy.17), channel_id=1, source_target_pairs={{0,4},{4,8},{8,12},{12,16},{16,20},{20,24},{24,28},{1,5},{5,9},{9,... | collective-permute-start | bytes 12488 | tf_op jit(solution)/shard_map/ppermute | solution.py:13
  67.1 6.7 %collective-permute-start.11 = (f32[8,130,1]{1,0,2:T(8,128)S(1)}, f32[8,130,1]{1,0,2:T(8,128)S(1)}, u32[]{:S(2)}, u32[]{:S(2)}) collective-permute-start(f32[8,130,1]{1,0,2:T(8,128)S(1)} %copy.19), channel_id=1, source_target_pairs={{4,0},{8,4},{12,8},{16,12},{20,16},{24,20},{28,24},{5,1},{9,5},{13... | collective-permute-start | bytes 12488 | tf_op jit(solution)/shard_map/ppermute | solution.py:16
  76.8 7.7 %copy-start = (f32[8,128,256]{2,0,1:T(8,128)}, f32[8,128,256]{2,0,1:T(8,128)S(1)}, u32[]{:S(2)}) copy-start(f32[8,128,256]{2,0,1:T(8,128)S(1)} %fusion.27) | copy-start | bytes 3145732
  76.8 6.2 %collective-permute-start.13 = (f32[8,1,256]{2,0,1:T(8,128)S(1)}, f32[8,1,256]{2,0,1:T(8,128)S(1)}, u32[]{:S(2)}, u32[]{:S(2)}) collective-permute-start(f32[8,1,256]{2,0,1:T(8,128)S(1)} %get-tuple-element.19), channel_id=1, source_target_pairs={{32,0},{64,32},{96,64},{128,96},{160,128},{192,160},{224,192},{33,... | collective-permute-start | bytes 24584 | tf_op jit(solution)/shard_map/ppermute | solution.py:16
  78.2 6.3 %collective-permute-start.12 = (f32[8,1,256]{2,0,1:T(8,128)S(1)}, f32[8,1,256]{2,0,1:T(8,128)S(1)}, u32[]{:S(2)}, u32[]{:S(2)}) collective-permute-start(f32[8,1,256]{2,0,1:T(8,128)S(1)} %get-tuple-element.20), channel_id=1, source_target_pairs={{0,32},{32,64},{64,96},{96,128},{128,160},{160,192},{192,224},{1,3... | collective-permute-start | bytes 24584 | tf_op jit(solution)/shard_map/ppermute | solution.py:13
  85.5 8.5 %copy-start.2 = (f32[5]{0:T(128)S(1)}, f32[5]{0:T(128)}, u32[]{:S(2)}) copy-start(f32[5]{0:T(128)} %param.9) | copy-start | bytes 64
  87.3 9.3 %collective-permute-start.15 = (f32[8,130,1]{1,0,2:T(8,128)S(1)}, f32[8,130,1]{1,0,2:T(8,128)S(1)}, u32[]{:S(2)}, u32[]{:S(2)}) collective-permute-start(f32[8,130,1]{1,0,2:T(8,128)S(1)} %copy.23), channel_id=1, source_target_pairs={{4,0},{8,4},{12,8},{16,12},{20,16},{24,20},{28,24},{5,1},{9,5},{13... | collective-permute-start | bytes 12488 | tf_op jit(solution)/shard_map/ppermute | solution.py:16
  88.6 6.8 %collective-permute-start.14 = (f32[8,130,1]{1,0,2:T(8,128)S(1)}, f32[8,130,1]{1,0,2:T(8,128)S(1)}, u32[]{:S(2)}, u32[]{:S(2)}) collective-permute-start(f32[8,130,1]{1,0,2:T(8,128)S(1)} %copy.21), channel_id=1, source_target_pairs={{0,4},{4,8},{8,12},{12,16},{16,20},{20,24},{24,28},{1,5},{5,9},{9,... | collective-permute-start | bytes 12488 | tf_op jit(solution)/shard_map/ppermute | solution.py:13
  106.1 7.3 %collective-permute-start.17 = (f32[8,1,256]{2,0,1:T(8,128)S(1)}, f32[8,1,256]{2,0,1:T(8,128)S(1)}, u32[]{:S(2)}, u32[]{:S(2)}) collective-permute-start(f32[8,1,256]{2,0,1:T(8,128)S(1)} %get-tuple-element.17), channel_id=1, source_target_pairs={{32,0},{64,32},{96,64},{128,96},{160,128},{192,160},{224,192},{33,... | collective-permute-start | bytes 24584 | tf_op jit(solution)/shard_map/ppermute | solution.py:16
  107.4 7.4 %collective-permute-start.16 = (f32[8,1,256]{2,0,1:T(8,128)S(1)}, f32[8,1,256]{2,0,1:T(8,128)S(1)}, u32[]{:S(2)}, u32[]{:S(2)}) collective-permute-start(f32[8,1,256]{2,0,1:T(8,128)S(1)} %get-tuple-element.18), channel_id=1, source_target_pairs={{0,32},{32,64},{64,96},{96,128},{128,160},{160,192},{192,224},{1,3... | collective-permute-start | bytes 24584 | tf_op jit(solution)/shard_map/ppermute | solution.py:13
  115.4 6.7 %collective-permute-start.18 = (f32[8,130,1]{1,0,2:T(8,128)S(1)}, f32[8,130,1]{1,0,2:T(8,128)S(1)}, u32[]{:S(2)}, u32[]{:S(2)}) collective-permute-start(f32[8,130,1]{1,0,2:T(8,128)S(1)} %copy.25), channel_id=1, source_target_pairs={{0,4},{4,8},{8,12},{12,16},{16,20},{20,24},{24,28},{1,5},{5,9},{9,... | collective-permute-start | bytes 12488 | tf_op jit(solution)/shard_map/ppermute | solution.py:13
  120.6 6.7 %collective-permute-start.19 = (f32[8,130,1]{1,0,2:T(8,128)S(1)}, f32[8,130,1]{1,0,2:T(8,128)S(1)}, u32[]{:S(2)}, u32[]{:S(2)}) collective-permute-start(f32[8,130,1]{1,0,2:T(8,128)S(1)} %copy.27), channel_id=1, source_target_pairs={{4,0},{8,4},{12,8},{16,12},{20,16},{24,20},{28,24},{5,1},{9,5},{13... | collective-permute-start | bytes 12488 | tf_op jit(solution)/shard_map/ppermute | solution.py:16
Sparse Core Ops, SparseCore 0:
  131.9 71.4 all-gather.1
